TPU v7x, 512 devices: a whole 4x4x16 slice. The times are simulated.
512 devices in a mesh: gx: 64 (over z, y), gz: 8 (over x, core).
Axes of the slice: x: 4, y: 4, z: 16, core: 2. Of those that a mesh axis runs over, the one named last changes fastest.
Arguments:
- tokens: bfloat16 [4, 256, 64, 768], P(None, 'gx', 'gz'), may hold values from -60 to 60
- cross_qkv: bfloat16 [768, 2304], P(None, 'gx'), may hold values from -16 to 16
- cross_out: bfloat16 [768, 768], P('gx'), may hold values from -0.21875 to 0.21875
- depth_qkv: bfloat16 [768, 2304], P(None, 'gx'), may hold values from -16 to 16
- depth_out: bfloat16 [768, 768], P('gx'), may hold values from -0.21875 to 0.21875
- up_proj: bfloat16 [768, 3072], P(None, 'gz'), may hold values from -0.21875 to 0.21875
- down_proj: bfloat16 [3072, 768], P('gz'), may hold values from -0.109375 to 0.109375
- gains: float32 [3, 768], replicated, may hold values from 0.5 to 1.5
- head_weight: float32 [768], replicated, may hold values from -0.21875 to 0.21875
- head_bias: float32 [1], replicated, may hold values from -1 to 1
Outputs:
- features: bfloat16 [4, 256, 64, 768], P(None, 'gx', 'gz')
- geotime: float32 [4, 256, 64], P(None, 'gx', 'gz')
All inputs are finite; a program needn't handle non-finite values.
Results may differ from a plain program's by a relative error of at most 0.013.
Values may be sent and summed in bfloat16 or wider, within the bound.
A program may use at most 64 MiB of HBM per device.

v0:
```python
import math
import jax
import jax.numpy as jnp
from jax import lax
from jax.sharding import PartitionSpec as P

HDIM = 64
log_span = math.log(256.0)


def carried_in(shard, axis, combine, identity):
    peers, position = (lax.axis_size(axis), lax.axis_index(axis))
    everything = lax.all_gather(shard, axis)
    start = jnp.broadcast_to(jnp.asarray(identity, shard.dtype), shard.shape)

    def step(k, before):
        reached = k < position
        new = combine(before, everything[k])
        return jnp.where(reached, new, before)

    return lax.fori_loop(0, peers, step, start)


def encodings(inlines, crosslines, depths, cross_start, depth_start, model_width):
    pairs = model_width // 2
    index = jnp.arange(pairs)
    freq = math.pi * jnp.exp(-log_span * index.astype(jnp.float32) / pairs)
    which = index % 3
    inline_pos = jnp.arange(inlines).astype(jnp.float32)[:, None, None, None]
    cross_pos = (cross_start + jnp.arange(crosslines)).astype(jnp.float32)[None, :, None, None]
    depth_pos = (depth_start + jnp.arange(depths)).astype(jnp.float32)[None, None, :, None]
    zeros = jnp.zeros((inlines, crosslines, depths, pairs), jnp.float32)
    position = jnp.where(
        which == 0, inline_pos + zeros, jnp.where(which == 1, cross_pos + zeros, depth_pos + zeros)
    )
    angle = position * freq
    return jnp.stack([jnp.sin(angle), jnp.cos(angle)], -1).reshape(
        inlines, crosslines, depths, model_width
    )


def normalize(stream, gain):
    scale = lax.rsqrt(jnp.mean(stream * stream, -1, keepdims=True) + 1e-05)
    return (stream * scale * gain).astype(jnp.bfloat16)


def attend(queries, keys, values):
    scale = queries.shape[-1] ** (-0.5)
    scores = (
        jnp.einsum("...qe,...ke->...qk", queries, keys, preferred_element_type=jnp.float32) * scale
    )
    scores = scores - jnp.max(scores, -1, keepdims=True)
    expo = jnp.exp(scores)
    weights = (expo / jnp.sum(expo, -1, keepdims=True)).astype(jnp.bfloat16)
    mixed = jnp.einsum("...qk,...ke->...qe", weights, values, preferred_element_type=jnp.float32)
    return mixed.astype(jnp.bfloat16)


def attend_items(trio):
    return attend(trio[0], trio[1], trio[2])


def body(
    tokens,
    cross_qkv,
    cross_out,
    depth_qkv,
    depth_out,
    up_proj,
    down_proj,
    gains,
    head_weight,
    head_bias,
):
    inlines, cross_dev, depth_dev, model_width = tokens.shape
    tok_rows = inlines * cross_dev * depth_dev
    head_count = model_width // HDIM
    cross_group = lax.axis_size("gx")
    encoding = encodings(
        inlines,
        cross_dev,
        depth_dev,
        lax.axis_index("gx") * cross_dev,
        lax.axis_index("gz") * depth_dev,
        model_width,
    )
    stream = (tokens.astype(jnp.float32) + encoding).reshape(tok_rows, model_width)
    normed = normalize(stream, gains[0])
    packed = jnp.dot(
        normed,
        lax.all_gather(cross_qkv, "gx", axis=1, tiled=True),
        preferred_element_type=jnp.float32,
    ).astype(jnp.bfloat16)
    packed = packed.reshape(inlines, cross_dev, depth_dev, 3, head_count, HDIM)
    lined = jnp.transpose(packed, (3, 0, 2, 4, 1, 5))
    per_item = inlines * depth_dev * head_count // cross_group
    lined = lined.reshape(3, cross_group, per_item, cross_dev, HDIM)
    mixed = attend_items(
        (
            lax.all_to_all(lined[0], "gx", split_axis=0, concat_axis=2, tiled=True),
            lax.all_to_all(lined[1], "gx", split_axis=0, concat_axis=2, tiled=True),
            lax.all_to_all(lined[2], "gx", split_axis=0, concat_axis=2, tiled=True),
        )
    )
    mixed = lax.all_to_all(mixed, "gx", split_axis=2, concat_axis=0, tiled=True)
    mixed = jnp.transpose(
        mixed.reshape(inlines, depth_dev, head_count, cross_dev, HDIM), (0, 3, 1, 2, 4)
    ).reshape(tok_rows, model_width)
    columns = mixed
    stream = stream + jnp.dot(
        columns,
        lax.all_gather(cross_out, "gx", axis=0, tiled=True),
        preferred_element_type=jnp.float32,
    )
    normed = normalize(stream, gains[1])
    packed = jnp.dot(
        normed,
        lax.all_gather(depth_qkv, "gx", axis=1, tiled=True),
        preferred_element_type=jnp.float32,
    ).astype(jnp.bfloat16)
    packed = packed.reshape(inlines, cross_dev, depth_dev, 3, head_count, HDIM)
    lined = jnp.transpose(packed, (3, 0, 1, 4, 2, 5))
    all_keys, all_values = (
        lax.all_gather(lined[1], "gz", axis=3, tiled=True),
        lax.all_gather(lined[2], "gz", axis=3, tiled=True),
    )
    mixed = attend(lined[0], all_keys, all_values)
    mixed = jnp.transpose(mixed, (0, 1, 3, 2, 4)).reshape(tok_rows, model_width)
    columns = mixed
    stream = stream + jnp.dot(
        columns,
        lax.all_gather(depth_out, "gx", axis=0, tiled=True),
        preferred_element_type=jnp.float32,
    )
    normed = normalize(stream, gains[2])
    hidden = jax.nn.gelu(
        jnp.dot(
            lax.all_gather(normed, "gz", axis=0, tiled=True),
            up_proj,
            preferred_element_type=jnp.float32,
        )
    ).astype(jnp.bfloat16)
    stream = stream + lax.psum_scatter(
        jnp.dot(hidden, down_proj, preferred_element_type=jnp.float32).astype(jnp.bfloat16),
        "gz",
        scatter_dimension=0,
        tiled=True,
    ).astype(jnp.float32)
    features = stream.astype(jnp.bfloat16).reshape(inlines, cross_dev, depth_dev, model_width)
    thickness = jax.nn.softplus(
        jnp.dot(stream, head_weight, precision=lax.Precision.HIGHEST) + head_bias[0]
    )
    local_time = jnp.cumsum(thickness.reshape(inlines, cross_dev, depth_dev), axis=2)
    line_total = local_time[:, :, -1]
    carried = carried_in(
        line_total, "gz", lambda earlier, later: earlier + later, jnp.zeros_like(line_total)
    )
    geotime = local_time + carried[:, :, None]
    return (features, geotime)


def solution(mesh):
    return jax.shard_map(
        body,
        mesh=mesh,
        in_specs=(
            P(None, "gx", "gz", None),
            P(None, "gx"),
            P("gx", None),
            P(None, "gx"),
            P("gx", None),
            P(None, "gz"),
            P("gz", None),
            P(),
            P(),
            P(),
        ),
        out_specs=(P(None, "gx", "gz", None), P(None, "gx", "gz")),
        check_vma=False,
    )
```

profile of v0, /device:TPU:1, one launch (start us, length us, event | category | flops | bytes accessed | tf_op | source)
XLA Modules:
  0.0 772.2 jit_solution(6534772506447443359)
XLA Ops:
  7.2 0.7 all-gather.21.cloned.1.call-update
  8.0 0.7 all-gather.23.cloned.1.call-update
  8.7 0.7 all-gather.25.cloned.1.call-update
  9.5 0.8 fusion.41
  10.3 6.4 copy.57
  16.6 4.4 copy.58
  21.4 132.3 %all-gather.21.cloned.1.call-done = bf16[64,36,768]{2,1,0:T(8,128)(2,1)} async-done(((bf16[1,36,768]{2,1,0:T(8,128)(2,1)}), bf16[64,36,768]{2,1,0:T(8,128)(2,1)}) %all-gather.21.cloned.1.call-update) | async-done | bytes 3538960 | tf_op jit(solution)/shard_map/all_gather | solution.py:91
  153.7 6.2 reshape.159
  159.8 3.3 convolution_convert_fusion.1
  163.1 1.0 reshape.145
  164.1 1.1 fusion.53
  165.3 0.3 copy.61
  165.6 0.9 reshape.175
  166.5 8.7 %all-to-all-start.1 = ((bf16[64,2,768]{2,1,0:T(2,128)(2,1)}), bf16[64,2,768]{2,1,0:T(2,128)(2,1)S(1)}, u32[]{:S(2)}, u32[]{:S(2)}) async-start(bf16[64,2,768]{2,1,0:T(2,128)(2,1)} %reshape.175), calls=%async_computation.1 | async-start | bytes 393216 | tf_op jit(solution)/shard_map/all_to_all | solution.py:101
  175.2 0.3 copy.59
  175.5 0.9 reshape.173
  176.5 15.4 %all-to-all-done.1 = bf16[64,2,768]{2,1,0:T(2,128)(2,1)S(1)} async-done(((bf16[64,2,768]{2,1,0:T(2,128)(2,1)}), bf16[64,2,768]{2,1,0:T(2,128)(2,1)S(1)}, u32[]{:S(2)}, u32[]{:S(2)}) %all-to-all-start.1) | async-done | bytes 196640 | tf_op jit(solution)/shard_map/all_to_all | solution.py:101
  191.9 4.6 all-to-all-start
  196.5 0.3 copy.65
  196.8 0.9 reshape.171
  197.7 15.1 %all-to-all-done = bf16[64,2,768]{2,1,0:T(2,128)(2,1)S(1)} async-done(((bf16[64,2,768]{2,1,0:T(2,128)(2,1)}), bf16[64,2,768]{2,1,0:T(2,128)(2,1)S(1)}, u32[]{:S(2)}, u32[]{:S(2)}) %all-to-all-start) | async-done | bytes 196640 | tf_op jit(solution)/shard_map/all_to_all | solution.py:100
  212.9 4.6 all-to-all-start.2
  217.5 0.5 all-gather.27.cloned.1.call-update
  218.1 0.3 reshape.176
  218.5 0.3 reshape.174
  218.9 15.0 %all-to-all-done.2 = bf16[64,2,768]{2,1,0:T(2,128)(2,1)S(1)} async-done(((bf16[64,2,768]{2,1,0:T(2,128)(2,1)}), bf16[64,2,768]{2,1,0:T(2,128)(2,1)S(1)}, u32[]{:S(2)}, u32[]{:S(2)}) %all-to-all-start.2) | async-done | bytes 196640 | tf_op jit(solution)/shard_map/all_to_all | solution.py:102
  234.4 1.8 fusion.55
  236.2 1.7 fusion.27
  237.9 0.3 copy.69
  238.2 1.0 reshape.177
  239.2 4.6 all-to-all-start.3
  244.1 49.5 %all-gather.23.cloned.1.call-done = bf16[64,12,768]{2,1,0:T(8,128)(2,1)} async-done(((bf16[1,12,768]{2,1,0:T(8,128)(2,1)}), bf16[64,12,768]{2,1,0:T(8,128)(2,1)}) %all-gather.23.cloned.1.call-update) | async-done | bytes 1179664 | tf_op jit(solution)/shard_map/all_gather | solution.py:112
  293.6 2.2 reshape.161
  295.9 142.8 %all-gather.25.cloned.1.call-done = bf16[64,36,768]{2,1,0:T(8,128)(2,1)} async-done(((bf16[1,36,768]{2,1,0:T(8,128)(2,1)}), bf16[64,36,768]{2,1,0:T(8,128)(2,1)}) %all-gather.25.cloned.1.call-update) | async-done | bytes 3538960 | tf_op jit(solution)/shard_map/all_gather | solution.py:118
  438.7 6.2 reshape.163
  444.9 0.3 reshape.178
  445.5 0.3 reshape.150
  445.8 0.4 multiply_reduce_fusion.1
  446.2 0.7 copy-done.1
  447.0 3.3 convolution_convert_fusion
  450.3 1.0 reshape.151
  451.3 0.3 copy.84
  451.6 1.0 fusion.54
  452.6 0.5 all-gather.19.cloned.1.call-update
  453.2 122.6 %all-gather.27.cloned.1.call-done = bf16[64,12,768]{2,1,0:T(8,128)(2,1)} async-done(((bf16[1,12,768]{2,1,0:T(8,128)(2,1)}), bf16[64,12,768]{2,1,0:T(8,128)(2,1)}) %all-gather.27.cloned.1.call-update) | async-done | bytes 1179664 | tf_op jit(solution)/shard_map/all_gather | solution.py:132
  575.8 2.2 reshape.165
  578.1 44.5 %all-gather.17.cloned.1.call-done = bf16[1,4,4,12,64,64]{5,4,3,2,1,0:T(8,128)(2,1)} async-done(((bf16[1,4,4,12,8,64]{5,4,3,2,1,0:T(8,128)(2,1)}), bf16[1,4,4,12,64,64]{5,4,3,2,1,0:T(8,128)(2,1)}) %all-gather.17.cloned.1.call-update) | async-done | bytes 1572880 | tf_op jit(solution)/shard_map/all_gather | solution.py:124
  622.5 4.6 fusion.56
  627.2 37.7 %all-gather.19.cloned.1.call-done = bf16[1,4,4,12,64,64]{5,4,3,2,1,0:T(8,128)(2,1)} async-done(((bf16[1,4,4,12,8,64]{5,4,3,2,1,0:T(8,128)(2,1)}), bf16[1,4,4,12,64,64]{5,4,3,2,1,0:T(8,128)(2,1)}) %all-gather.19.cloned.1.call-update) | async-done | bytes 1572880 | tf_op jit(solution)/shard_map/all_gather | solution.py:125
  664.9 3.1 fusion.24
  668.2 0.3 reshape.152
  668.5 0.6 copy-done.2
  669.0 0.4 multiply_reduce_fusion
  669.5 0.8 multiply_convert_fusion
  670.3 33.1 %all-gather.15.cloned.1.call-done = bf16[1024,768]{1,0:T(8,128)(2,1)} async-done(((bf16[128,768]{1,0:T(8,128)(2,1)}), bf16[1024,768]{1,0:T(8,128)(2,1)}) %all-gather.15.cloned.1.call-update) | async-done | bytes 1572880 | tf_op jit(solution)/shard_map/all_gather | solution.py:138
  703.5 4.6 convolution_convert_fusion.2
  708.2 0.7 copy-done.6
  709.5 37.5 %reduce-scatter.2.cloned.1.call-done = bf16[128,768]{1,0:T(8,128)(2,1)} async-done(((bf16[1024,768]{1,0:T(8,128)(2,1)}), bf16[128,768]{1,0:T(8,128)(2,1)}) %reduce-scatter.2.cloned.1.call-update) | async-done | bytes 196624 | tf_op jit(solution)/shard_map/reduce_scatter | solution.py:143
  747.0 1.4 compare_select_fusion
  748.4 0.7 reduce_window_sum.11
  749.3 13.5 %all-gather.2 = f32[32,4,1]{1,2,0:T(1,128)S(1)} all-gather(f32[4,4,1]{1,2,0:T(1,128)S(1)} %copy.75), channel_id=4, replica_groups=mesh['gx'=64,'gz'=8] {'gz'}, dimensions={0}, use_global_device_ids=true | all-gather | bytes 576 | tf_op jit(solution)/shard_map/all_gather | solution.py:13
  762.8 0.3 while.14
  763.1 0.7 broadcast_add_fusion
  763.8 1.6 fusion.37
  (56 shorter events, 2.5 us)
Async XLA Ops:
  7.2 696.3 %copy-start = (bf16[384,768]{1,0:T(8,128)(2,1)S(1)}, bf16[384,768]{1,0:T(8,128)(2,1)}, u32[]{:S(2)}) copy-start(bf16[384,768]{1,0:T(8,128)(2,1)} %param.18) | copy-start | bytes 1769476
  7.2 146.5 %all-gather.21.cloned.1.call-start = ((), (), s32[]{:S(2)}) async-start(), calls=%async_computation.9 | async-start | bytes 3993600 | tf_op jit(solution)/shard_map/all_gather | solution.py:91
  7.9 285.7 %all-gather.23.cloned.1.call-start = ((), (), s32[]{:S(2)}) async-start(), calls=%async_computation.10 | async-start | bytes 1597440 | tf_op jit(solution)/shard_map/all_gather | solution.py:112
  8.7 430.0 %all-gather.25.cloned.1.call-start = ((), (), s32[]{:S(2)}) async-start(), calls=%async_computation.11 | async-start | bytes 3993600 | tf_op jit(solution)/shard_map/all_gather | solution.py:118
  16.6 4.4 copy-start.4
  16.6 4.6 copy-start.5
  165.2 10.0 %copy-start.3 = (bf16[1,4,8,12,4,64]{5,3,0,2,4,1:T(8,128)(2,1)S(1)}, bf16[1,4,8,12,4,64]{5,3,0,2,4,1:T(8,128)(2,1)}, u32[]{:S(2)}) copy-start(bf16[1,4,8,12,4,64]{5,3,0,2,4,1:T(8,128)(2,1)} %get-tuple-element.128) | copy-start | bytes 589828
  166.5 25.4 %all-to-all-start.1 = ((bf16[64,2,768]{2,1,0:T(2,128)(2,1)}), bf16[64,2,768]{2,1,0:T(2,128)(2,1)S(1)}, u32[]{:S(2)}, u32[]{:S(2)}) async-start(bf16[64,2,768]{2,1,0:T(2,128)(2,1)} %reshape.175), calls=%async_computation.1 | async-start | bytes 393216 | tf_op jit(solution)/shard_map/all_to_all | solution.py:101
  191.9 21.0 %all-to-all-start = ((bf16[64,2,768]{2,1,0:T(2,128)(2,1)}), bf16[64,2,768]{2,1,0:T(2,128)(2,1)S(1)}, u32[]{:S(2)}, u32[]{:S(2)}) async-start(bf16[64,2,768]{2,1,0:T(2,128)(2,1)} %reshape.173), calls=%async_computation | async-start | bytes 393216 | tf_op jit(solution)/shard_map/all_to_all | solution.py:100
  212.9 21.1 %all-to-all-start.2 = ((bf16[64,2,768]{2,1,0:T(2,128)(2,1)}), bf16[64,2,768]{2,1,0:T(2,128)(2,1)S(1)}, u32[]{:S(2)}, u32[]{:S(2)}) async-start(bf16[64,2,768]{2,1,0:T(2,128)(2,1)} %reshape.171), calls=%async_computation.2 | async-start | bytes 393216 | tf_op jit(solution)/shard_map/all_to_all | solution.py:102
  217.5 358.3 %all-gather.27.cloned.1.call-start = ((), (), s32[]{:S(2)}) async-start(), calls=%async_computation.12 | async-start | bytes 1597440 | tf_op jit(solution)/shard_map/all_gather | solution.py:132
  239.2 205.6 %all-to-all-start.3 = ((bf16[64,2,768]{2,1,0:T(2,128)(2,1)}), bf16[64,2,768]{2,1,0:T(2,128)(2,1)S(1)}, u32[]{:S(2)}, u32[]{:S(2)}) async-start(bf16[64,2,768]{2,1,0:T(2,128)(2,1)} %reshape.177), calls=%async_computation.3 | async-start | bytes 393216 | tf_op jit(solution)/shard_map/all_to_all | solution.py:105
  243.9 378.7 %all-gather.17.cloned.1.call-start = ((), (), s32[]{:S(2)}) async-start(), calls=%async_computation.7 | async-start | bytes 3538944 | tf_op jit(solution)/shard_map/all_gather | solution.py:124
  446.2 0.7 copy-start.1
  452.6 212.3 %all-gather.19.cloned.1.call-start = ((), (), s32[]{:S(2)}) async-start(), calls=%async_computation.8 | async-start | bytes 3538944 | tf_op jit(solution)/shard_map/all_gather | solution.py:125
  453.2 250.3 %all-gather.15.cloned.1.call-start = ((), (), s32[]{:S(2)}) async-start(), calls=%async_computation.5 | async-start | bytes 1769472 | tf_op jit(solution)/shard_map/all_gather | solution.py:138
  668.0 1.0 copy-start.2
  670.3 76.7 %reduce-scatter.2.cloned.1.call-start = ((), (), s32[]{:S(2)}) async-start(), calls=%async_computation.6 | async-start | bytes 1769472 | tf_op jit(solution)/shard_map/reduce_scatter | solution.py:143
  708.1 0.7 copy-start.6
Sparse Core Ops, SparseCore 0:
  11.0 142.6 all-gather.20
  156.6 136.9 all-gather.22
  296.6 142.0 all-gather.24
  441.5 134.2 all-gather.26
  577.8 44.7 all-gather.16
  624.5 40.3 all-gather.18
  670.4 33.0 all-gather.14
  708.3 38.6 reduce-scatter.1
where the time goes:
time: 773 us; the launch traced here: 772 us
  waiting for transfers between devices  649 us (84%)
  local copies, waits for them, and re-layouts  41.9 us (5%)
  matrix products  24.7 us (3%)
  starting transfers between devices  23.1 us (3%)
  between operations  15.2 us (2%)
  blocking collectives  13.5 us (2%)
    all_gather x1, waiting for transfers between devices, body(): lax.all_gather(depth_qkv, 'gx', axis=1, tiled=True)  143 us
    all_gather x1, waiting for transfers between devices, body(): lax.all_gather(cross_qkv, 'gx', axis=1, tiled=True)  132 us
    all_gather x1, waiting for transfers between devices, body(): lax.all_gather(depth_out, 'gx', axis=0, tiled=True)  123 us
    all_gather x1, waiting for transfers between devices, body(): lax.all_gather(cross_out, 'gx', axis=0, tiled=True)  49.5 us
    all_gather x1, waiting for transfers between devices, body(): lax.all_gather(lined[1], 'gz', axis=3, tiled=True)  44.5 us
    all_gather x1, waiting for transfers between devices, body(): lax.all_gather(lined[2], 'gz', axis=3, tiled=True)  37.7 us
    reduce_scatter x1, waiting for transfers between devices, body(): lax.psum_scatter(jnp.dot(hidden, down_proj, preferred_element_type=jnp.fl...  37.5 us
    all_gather x1, waiting for transfers between devices, body(): lax.all_gather(normed, 'gz', axis=0, tiled=True)  33.1 us
  transfers between devices with their start and end apart: 12, of which 11 were waited for; matrix products, arithmetic and copies ran while one was open for 7% of the time, Pallas kernels for 0%

commit v1 on v0

--- a/solution.py
+++ b/solution.py
@@ -6,6 +6,12 @@
 
 HDIM = 64
 log_span = math.log(256.0)
+
+
+def link_node(local_array, mesh_ax, row_dim, axis_k):
+    x_new = jnp.split(local_array, jax.lax.axis_size(mesh_ax), axis=row_dim)
+    fresh = jax.lax.all_to_all(jnp.stack(x_new), axis_name=mesh_ax, split_axis=0, concat_axis=0)
+    return jnp.concatenate(fresh, axis=axis_k)
 
 
 def carried_in(shard, axis, combine, identity):
@@ -99,7 +105,7 @@
         (
             lax.all_to_all(lined[0], "gx", split_axis=0, concat_axis=2, tiled=True),
             lax.all_to_all(lined[1], "gx", split_axis=0, concat_axis=2, tiled=True),
-            lax.all_to_all(lined[2], "gx", split_axis=0, concat_axis=2, tiled=True),
+            link_node(lined[2], "gx", 0, axis_k=2),
         )
     )
     mixed = lax.all_to_all(mixed, "gx", split_axis=2, concat_axis=0, tiled=True)

time: 773 us -> 773 us (level)
    unnamed x27 -> x90, local copies, waits for them, and re-layouts: 23.7 us -> 24.5 us
where the time goes in v1:
time: 773 us; the launch traced here: 772 us
  waiting for transfers between devices  648 us (84%)
  local copies, waits for them, and re-layouts  42.6 us (6%)
  matrix products  24.7 us (3%)
  starting transfers between devices  23.1 us (3%)
  between operations  15.4 us (2%)
  blocking collectives  13.4 us (2%)
    all_gather x1, waiting for transfers between devices, body(): lax.all_gather(depth_qkv, 'gx', axis=1, tiled=True)  143 us
    all_gather x1, waiting for transfers between devices, body(): lax.all_gather(cross_qkv, 'gx', axis=1, tiled=True)  132 us
    all_gather x1, waiting for transfers between devices, body(): lax.all_gather(depth_out, 'gx', axis=0, tiled=True)  123 us
    all_gather x1, waiting for transfers between devices, body(): lax.all_gather(cross_out, 'gx', axis=0, tiled=True)  48.2 us
    all_gather x1, waiting for transfers between devices, body(): lax.all_gather(lined[1], 'gz', axis=3, tiled=True)  44.5 us
    all_gather x1, waiting for transfers between devices, body(): lax.all_gather(lined[2], 'gz', axis=3, tiled=True)  37.7 us
    reduce_scatter x1, waiting for transfers between devices, body(): lax.psum_scatter(jnp.dot(hidden, down_proj, preferred_element_type=jnp.fl...  37.5 us
    all_gather x1, waiting for transfers between devices, body(): lax.all_gather(normed, 'gz', axis=0, tiled=True)  33.1 us
  transfers between devices with their start and end apart: 12, of which 11 were waited for; matrix products, arithmetic and copies ran while one was open for 7% of the time, Pallas kernels for 0%

profile of v1, /device:TPU:1, one launch (start us, length us, event | category | flops | bytes accessed | tf_op | source)
XLA Modules:
  0.0 772.0 jit_solution(13893064907834304056)
XLA Ops:
  7.2 0.7 all-gather.21.cloned.1.call-update
  8.0 0.7 all-gather.23.cloned.1.call-update
  8.7 0.7 all-gather.25.cloned.1.call-update
  9.5 0.8 fusion.41
  10.3 6.4 copy.120
  16.6 4.4 copy.121
  21.4 132.3 %all-gather.21.cloned.1.call-done = bf16[64,36,768]{2,1,0:T(8,128)(2,1)} async-done(((bf16[1,36,768]{2,1,0:T(8,128)(2,1)}), bf16[64,36,768]{2,1,0:T(8,128)(2,1)}) %all-gather.21.cloned.1.call-update) | async-done | bytes 3538960 | tf_op jit(solution)/shard_map/all_gather | solution.py:97
  153.7 6.2 reshape.164
  159.8 3.3 convolution_convert_fusion.1
  163.1 1.0 reshape.149
  164.1 1.1 fusion.53
  165.2 0.3 copy.128
  166.6 0.9 reshape.176
  167.5 8.7 %all-to-all-start.2 = ((bf16[64,2,768]{2,1,0:T(2,128)(2,1)}), bf16[64,2,768]{2,1,0:T(2,128)(2,1)S(1)}, u32[]{:S(2)}, u32[]{:S(2)}) async-start(bf16[64,2,768]{2,1,0:T(2,128)(2,1)} %reshape.176), calls=%async_computation.2 | async-start | bytes 393216 | tf_op jit(solution)/shard_map/all_to_all | solution.py:13
  176.2 0.3 copy.124
  176.5 0.9 reshape.180
  177.5 15.4 %all-to-all-done.2 = bf16[64,2,768]{2,1,0:T(2,128)(2,1)S(1)} async-done(((bf16[64,2,768]{2,1,0:T(2,128)(2,1)}), bf16[64,2,768]{2,1,0:T(2,128)(2,1)S(1)}, u32[]{:S(2)}, u32[]{:S(2)}) %all-to-all-start.2) | async-done | bytes 196640 | tf_op jit(solution)/shard_map/all_to_all | solution.py:13
  192.9 4.6 all-to-all-start.1
  197.5 0.3 copy.122
  197.8 0.9 reshape.178
  198.8 15.3 %all-to-all-done.1 = bf16[64,2,768]{2,1,0:T(2,128)(2,1)S(1)} async-done(((bf16[64,2,768]{2,1,0:T(2,128)(2,1)}), bf16[64,2,768]{2,1,0:T(2,128)(2,1)S(1)}, u32[]{:S(2)}, u32[]{:S(2)}) %all-to-all-start.1) | async-done | bytes 196640 | tf_op jit(solution)/shard_map/all_to_all | solution.py:107
  214.1 4.6 all-to-all-start
  218.7 0.5 all-gather.27.cloned.1.call-update
  219.3 0.3 reshape.177
  219.7 0.3 reshape.181
  220.1 15.1 %all-to-all-done = bf16[64,2,768]{2,1,0:T(2,128)(2,1)S(1)} async-done(((bf16[64,2,768]{2,1,0:T(2,128)(2,1)}), bf16[64,2,768]{2,1,0:T(2,128)(2,1)S(1)}, u32[]{:S(2)}, u32[]{:S(2)}) %all-to-all-start) | async-done | bytes 196640 | tf_op jit(solution)/shard_map/all_to_all | solution.py:106
  235.7 1.8 fusion.55
  237.5 1.7 fusion.27
  239.2 0.3 copy.132
  239.5 1.0 reshape.182
  240.5 4.8 all-to-all-start.3
  245.4 48.2 %all-gather.23.cloned.1.call-done = bf16[64,12,768]{2,1,0:T(8,128)(2,1)} async-done(((bf16[1,12,768]{2,1,0:T(8,128)(2,1)}), bf16[64,12,768]{2,1,0:T(8,128)(2,1)}) %all-gather.23.cloned.1.call-update) | async-done | bytes 1179664 | tf_op jit(solution)/shard_map/all_gather | solution.py:118
  293.5 2.2 reshape.166
  295.8 142.7 %all-gather.25.cloned.1.call-done = bf16[64,36,768]{2,1,0:T(8,128)(2,1)} async-done(((bf16[1,36,768]{2,1,0:T(8,128)(2,1)}), bf16[64,36,768]{2,1,0:T(8,128)(2,1)}) %all-gather.25.cloned.1.call-update) | async-done | bytes 3538960 | tf_op jit(solution)/shard_map/all_gather | solution.py:124
  438.5 6.2 reshape.168
  444.6 0.3 reshape.183
  445.3 0.3 reshape.155
  445.6 0.4 multiply_reduce_fusion.1
  446.0 0.7 copy-done.1
  446.7 3.3 convolution_convert_fusion
  450.0 1.0 reshape.156
  451.0 0.3 copy.147
  451.3 1.0 fusion.54
  452.4 0.5 all-gather.19.cloned.1.call-update
  453.0 122.6 %all-gather.27.cloned.1.call-done = bf16[64,12,768]{2,1,0:T(8,128)(2,1)} async-done(((bf16[1,12,768]{2,1,0:T(8,128)(2,1)}), bf16[64,12,768]{2,1,0:T(8,128)(2,1)}) %all-gather.27.cloned.1.call-update) | async-done | bytes 1179664 | tf_op jit(solution)/shard_map/all_gather | solution.py:138
  575.6 2.2 reshape.170
  577.8 44.5 %all-gather.17.cloned.1.call-done = bf16[1,4,4,12,64,64]{5,4,3,2,1,0:T(8,128)(2,1)} async-done(((bf16[1,4,4,12,8,64]{5,4,3,2,1,0:T(8,128)(2,1)}), bf16[1,4,4,12,64,64]{5,4,3,2,1,0:T(8,128)(2,1)}) %all-gather.17.cloned.1.call-update) | async-done | bytes 1572880 | tf_op jit(solution)/shard_map/all_gather | solution.py:130
  622.3 4.6 fusion.56
  626.9 37.7 %all-gather.19.cloned.1.call-done = bf16[1,4,4,12,64,64]{5,4,3,2,1,0:T(8,128)(2,1)} async-done(((bf16[1,4,4,12,8,64]{5,4,3,2,1,0:T(8,128)(2,1)}), bf16[1,4,4,12,64,64]{5,4,3,2,1,0:T(8,128)(2,1)}) %all-gather.19.cloned.1.call-update) | async-done | bytes 1572880 | tf_op jit(solution)/shard_map/all_gather | solution.py:131
  664.7 3.1 fusion.24
  668.0 0.3 reshape.157
  668.3 0.6 copy-done.2
  668.8 0.4 multiply_reduce_fusion
  669.3 0.8 multiply_convert_fusion
  670.1 33.1 %all-gather.15.cloned.1.call-done = bf16[1024,768]{1,0:T(8,128)(2,1)} async-done(((bf16[128,768]{1,0:T(8,128)(2,1)}), bf16[1024,768]{1,0:T(8,128)(2,1)}) %all-gather.15.cloned.1.call-update) | async-done | bytes 1572880 | tf_op jit(solution)/shard_map/all_gather | solution.py:144
  703.3 4.6 convolution_convert_fusion.2
  707.9 0.7 copy-done.6
  709.2 37.5 %reduce-scatter.2.cloned.1.call-done = bf16[128,768]{1,0:T(8,128)(2,1)} async-done(((bf16[1024,768]{1,0:T(8,128)(2,1)}), bf16[128,768]{1,0:T(8,128)(2,1)}) %reduce-scatter.2.cloned.1.call-update) | async-done | bytes 196624 | tf_op jit(solution)/shard_map/reduce_scatter | solution.py:149
  746.8 1.4 compare_select_fusion
  748.2 0.7 reduce_window_sum.11
  749.1 13.4 %all-gather.2 = f32[32,4,1]{1,2,0:T(1,128)S(1)} all-gather(f32[4,4,1]{1,2,0:T(1,128)S(1)} %copy.138), channel_id=4, replica_groups=mesh['gx'=64,'gz'=8] {'gz'}, dimensions={0}, use_global_device_ids=true | all-gather | bytes 576 | tf_op jit(solution)/shard_map/all_gather | solution.py:19
  762.5 0.3 while.14
  762.8 0.7 broadcast_add_fusion
  763.5 1.6 fusion.37
  (120 shorter events, 3.1 us)
Async XLA Ops:
  7.2 696.1 %copy-start = (bf16[384,768]{1,0:T(8,128)(2,1)S(1)}, bf16[384,768]{1,0:T(8,128)(2,1)}, u32[]{:S(2)}) copy-start(bf16[384,768]{1,0:T(8,128)(2,1)} %param.18) | copy-start | bytes 1769476
  7.2 146.5 %all-gather.21.cloned.1.call-start = ((), (), s32[]{:S(2)}) async-start(), calls=%async_computation.9 | async-start | bytes 3993600 | tf_op jit(solution)/shard_map/all_gather | solution.py:97
  7.9 285.6 %all-gather.23.cloned.1.call-start = ((), (), s32[]{:S(2)}) async-start(), calls=%async_computation.10 | async-start | bytes 1597440 | tf_op jit(solution)/shard_map/all_gather | solution.py:118
  8.7 429.8 %all-gather.25.cloned.1.call-start = ((), (), s32[]{:S(2)}) async-start(), calls=%async_computation.11 | async-start | bytes 3993600 | tf_op jit(solution)/shard_map/all_gather | solution.py:124
  16.6 4.4 copy-start.4
  16.6 4.6 copy-start.5
  165.2 11.0 %copy-start.3 = (bf16[1,4,8,12,4,64]{5,3,0,2,4,1:T(8,128)(2,1)S(1)}, bf16[1,4,8,12,4,64]{5,3,0,2,4,1:T(8,128)(2,1)}, u32[]{:S(2)}) copy-start(bf16[1,4,8,12,4,64]{5,3,0,2,4,1:T(8,128)(2,1)} %get-tuple-element.126) | copy-start | bytes 589828
  167.5 25.4 %all-to-all-start.2 = ((bf16[64,2,768]{2,1,0:T(2,128)(2,1)}), bf16[64,2,768]{2,1,0:T(2,128)(2,1)S(1)}, u32[]{:S(2)}, u32[]{:S(2)}) async-start(bf16[64,2,768]{2,1,0:T(2,128)(2,1)} %reshape.176), calls=%async_computation.2 | async-start | bytes 393216 | tf_op jit(solution)/shard_map/all_to_all | solution.py:13
  192.9 21.2 %all-to-all-start.1 = ((bf16[64,2,768]{2,1,0:T(2,128)(2,1)}), bf16[64,2,768]{2,1,0:T(2,128)(2,1)S(1)}, u32[]{:S(2)}, u32[]{:S(2)}) async-start(bf16[64,2,768]{2,1,0:T(2,128)(2,1)} %reshape.180), calls=%async_computation.1 | async-start | bytes 393216 | tf_op jit(solution)/shard_map/all_to_all | solution.py:107
  214.1 21.2 %all-to-all-start = ((bf16[64,2,768]{2,1,0:T(2,128)(2,1)}), bf16[64,2,768]{2,1,0:T(2,128)(2,1)S(1)}, u32[]{:S(2)}, u32[]{:S(2)}) async-start(bf16[64,2,768]{2,1,0:T(2,128)(2,1)} %reshape.178), calls=%async_computation | async-start | bytes 393216 | tf_op jit(solution)/shard_map/all_to_all | solution.py:106
  218.7 356.9 %all-gather.27.cloned.1.call-start = ((), (), s32[]{:S(2)}) async-start(), calls=%async_computation.12 | async-start | bytes 1597440 | tf_op jit(solution)/shard_map/all_gather | solution.py:138
  240.5 204.1 %all-to-all-start.3 = ((bf16[64,2,768]{2,1,0:T(2,128)(2,1)}), bf16[64,2,768]{2,1,0:T(2,128)(2,1)S(1)}, u32[]{:S(2)}, u32[]{:S(2)}) async-start(bf16[64,2,768]{2,1,0:T(2,128)(2,1)} %reshape.182), calls=%async_computation.3 | async-start | bytes 393216 | tf_op jit(solution)/shard_map/all_to_all | solution.py:111
  245.3 377.0 %all-gather.17.cloned.1.call-start = ((), (), s32[]{:S(2)}) async-start(), calls=%async_computation.7 | async-start | bytes 3538944 | tf_op jit(solution)/shard_map/all_gather | solution.py:130
  446.0 0.7 copy-start.1
  452.4 212.3 %all-gather.19.cloned.1.call-start = ((), (), s32[]{:S(2)}) async-start(), calls=%async_computation.8 | async-start | bytes 3538944 | tf_op jit(solution)/shard_map/all_gather | solution.py:131
  452.9 250.3 %all-gather.15.cloned.1.call-start = ((), (), s32[]{:S(2)}) async-start(), calls=%async_computation.5 | async-start | bytes 1769472 | tf_op jit(solution)/shard_map/all_gather | solution.py:144
  667.8 1.0 copy-start.2
  670.1 76.7 %reduce-scatter.2.cloned.1.call-start = ((), (), s32[]{:S(2)}) async-start(), calls=%async_computation.6 | async-start | bytes 1769472 | tf_op jit(solution)/shard_map/reduce_scatter | solution.py:149
  707.9 0.7 copy-start.6
Sparse Core Ops, SparseCore 0:
  11.0 142.6 all-gather.20
  156.6 136.8 all-gather.22
  296.5 141.9 all-gather.24
  441.3 134.2 all-gather.26
  577.5 44.7 all-gather.16
  624.3 40.3 all-gather.18
  670.2 33.0 all-gather.14
  708.1 38.6 reduce-scatter.1
